TPU v7x, 256 devices: a whole 4x4x8 slice. The times are simulated.
256 devices in a mesh: leaf: 8 (over x, core), rows: 32 (over z, y).
Axes of the slice: x: 4, y: 4, z: 8, core: 2. Of those that a mesh axis runs over, the one named last changes fastest.
Arguments:
- leaf_inverse: bfloat16 [16384, 2048], P(('leaf', 'rows')), may hold values from -0.125 to 0.125
- leaf_panel: bfloat16 [245760, 2048], P(('leaf', 'rows')), may hold values from -0.0625 to 0.0625
- mid_inverse: bfloat16 [8192, 2048], P(('leaf', 'rows')), may hold values from -0.125 to 0.125
- mid_panel: bfloat16 [122880, 2048], P(('leaf', 'rows')), may hold values from -0.0625 to 0.0625
- top_inverse: bfloat16 [4096, 2048], P(('leaf', 'rows')), may hold values from -0.125 to 0.125
- top_panel: bfloat16 [61440, 2048], P(('leaf', 'rows')), may hold values from -0.0625 to 0.0625
- leaf_rhs: bfloat16 [128, 16384], P(None, ('leaf', 'rows')), may hold values from -6 to 6
- mid_rhs: bfloat16 [128, 8192], P(None, ('leaf', 'rows')), may hold values from -6 to 6
- top_rhs: bfloat16 [128, 4096], P(None, ('leaf', 'rows')), may hold values from -6 to 6
- outer_solution: bfloat16 [128, 61440], P(None, ('leaf', 'rows')), may hold values from -6 to 6
- leaf_targets: int32 [8, 240], replicated, may hold values from -1 to 255, as said below
- mid_targets: int32 [4, 240], replicated, may hold values from -1 to 255, as said below
- front_counts: int32 [14, 2], replicated, may hold values from 128 to 30720, as said below
Outputs:
- leaf_solution: bfloat16 [128, 16384], P(None, ('leaf', 'rows'))
- mid_solution: bfloat16 [128, 8192], P(None, ('leaf', 'rows'))
- top_solution: bfloat16 [128, 4096], P(None, ('leaf', 'rows'))
- top_contribution: bfloat16 [128, 61440], P(None, ('leaf', 'rows'))
Inputs may be any that keep to these rules, and one draw needn't show every extreme that they name: `front_counts`: row f gives a front's live pivot count and live update row count, leaf fronts first, then middle, then top fronts. Both are positive multiples of 128, at most 2048 and 30720; top front 0 has 2048 pivots and 30720 update rows. A child's update blocks never outnumber its parent's live blocks. `leaf_targets`: row c lists, for each update block j of leaf front c below its live update rows / 128, the block of middle front c // 2 that receives it, and -1 for the other j. The listed blocks are strictly increasing and live in the parent: below its pivot count / 128, or from 16 up to that plus its update rows / 128. `mid_targets`: row c lists, for each update block j of middle front c below its live update rows / 128, the block of top front c // 2 that receives it, and -1 for the other j. The listed blocks are strictly increasing and live in the parent, as for leaf_targets.
All inputs are finite; a program needn't handle non-finite values.
Results may differ from a plain program's by a relative error of at most 0.019.
Values may be sent and summed in bfloat16 or wider, within the bound.
A program may use at most 64 MiB of HBM per device.

v0:
```python
import jax
import jax.numpy as jnp
from jax import lax
from jax.sharding import PartitionSpec as P

FRONT_ROWS = 32768
PIVOTS = 2048
UPDATES = 30720


def from_partner(value, axis, stride):
    mask = 2**stride
    pairs = [(source, source ^ mask) for source in range(lax.axis_size(axis))]
    return lax.ppermute(value, axis, pairs)


def share_sections(piece_part, height, within):
    if height == 0:
        return piece_part
    current = piece_part
    for bit_index in range(height):
        partner = from_partner(current, "leaf", bit_index)
        upper_bit = within // (1 << bit_index) % 2
        lower_first = jnp.concatenate([current, partner], axis=1)
        upper_first = jnp.concatenate([partner, current], axis=1)
        current = jnp.where(upper_bit == 0, lower_first, upper_first)
    return current


def total_sections(partials, height, within):
    if height == 0:
        return partials[:, 0]
    current = partials
    for bit_index in reversed(range(height)):
        halves = current.reshape(current.shape[0], 2, current.shape[1] // 2, current.shape[2])
        upper_bit = within // (1 << bit_index) % 2
        keeping = lax.dynamic_index_in_dim(halves, upper_bit, 1, keepdims=False)
        sending = lax.dynamic_index_in_dim(halves, 1 - upper_bit, 1, keepdims=False)
        current = keeping + from_partner(sending.astype(jnp.bfloat16), "leaf", bit_index).astype(
            sending.dtype
        )
    return current[:, 0]


def place_level(height, section, row_index, row_count):
    group_width = 1 << height
    within = section % group_width
    front_index = section // group_width
    member = within * row_count + row_index
    return (group_width, within, front_index, member)


def live_rows(member, length, count):
    return (member * length + jnp.arange(length) < count)[None, :]


def block_onehot(targets, front_index, start_block, slab_blocks):
    target_row = lax.dynamic_index_in_dim(targets, front_index, 0, keepdims=False)
    target_row = lax.dynamic_slice_in_dim(target_row, start_block, slab_blocks)
    return (target_row[:, None] == jnp.arange(FRONT_ROWS // 128)[None, :]).astype(jnp.bfloat16)


def extend_children(update, height, targets, section, row_index, row_count):
    group_width, within, front_index, member = place_level(height, section, row_index, row_count)
    slab = lax.all_to_all(update, "rows", split_axis=0, concat_axis=1, tiled=True)
    narrow = slab.shape[0]
    slab_blocks = slab.shape[1] // 128
    onehot = block_onehot(targets, front_index, within * slab_blocks, slab_blocks)
    spread = jnp.einsum(
        "cjr,jb->cbr",
        slab.reshape(narrow, slab_blocks, 128),
        onehot,
        preferred_element_type=jnp.float32,
    )
    parent_width = 2 * group_width
    flattened = spread.reshape(narrow, FRONT_ROWS)
    pivot_side = flattened[:, :PIVOTS].reshape(narrow, parent_width, row_count, -1)
    update_side = flattened[:, PIVOTS:].reshape(narrow, parent_width, row_count, -1)
    joined = jnp.concatenate([pivot_side, update_side], axis=3).reshape(narrow, parent_width, -1)
    returned = lax.all_to_all(
        joined.astype(jnp.bfloat16), "rows", split_axis=2, concat_axis=0, tiled=True
    ).astype(joined.dtype)
    return total_sections(returned, height + 1, section % parent_width)


def descend_children(full_local, height, targets, section, row_count, pivot_local):
    group_width = 1 << height
    within = section % group_width
    columns_form = lax.all_to_all(full_local, "rows", split_axis=0, concat_axis=1, tiled=True)
    narrow = columns_form.shape[0]
    shared = share_sections(columns_form[:, None, :], height, within)
    parted = shared.reshape(narrow, group_width, row_count, -1)
    parent_full = jnp.concatenate(
        [
            parted[..., :pivot_local].reshape(narrow, PIVOTS),
            parted[..., pivot_local:].reshape(narrow, UPDATES),
        ],
        axis=1,
    )
    child_width = group_width // 2
    child_within = section % child_width
    child_front = section // child_width
    slab_blocks = UPDATES // (child_width * 128)
    onehot = block_onehot(targets, child_front, child_within * slab_blocks, slab_blocks)
    picked = jnp.einsum(
        "cbr,jb->cjr",
        parent_full.reshape(narrow, FRONT_ROWS // 128, 128),
        onehot,
        preferred_element_type=jnp.float32,
    )
    picked = picked.reshape(narrow, slab_blocks * 128).astype(jnp.bfloat16)
    return lax.all_to_all(picked, "rows", split_axis=1, concat_axis=0, tiled=True)


def separate_sums(partials, group_width, height, within):
    shaped = partials.reshape(partials.shape[0], group_width, -1)
    summed = lax.psum_scatter(
        shaped.astype(jnp.bfloat16), "rows", scatter_dimension=2, tiled=True
    ).astype(jnp.float32)
    return total_sections(summed, height, within)


def body(
    leaf_inverse,
    leaf_panel,
    mid_inverse,
    mid_panel,
    top_inverse,
    top_panel,
    leaf_rhs,
    mid_rhs,
    top_rhs,
    outer_solution,
    leaf_targets,
    mid_targets,
    front_counts,
):
    row_count = lax.axis_size("rows")
    leaf_count = lax.axis_size("leaf")
    section = lax.axis_index("leaf")
    row_index = lax.axis_index("rows")
    inverses = (leaf_inverse, mid_inverse, top_inverse)
    panels = (leaf_panel, mid_panel, top_panel)
    sources = (leaf_rhs, mid_rhs, top_rhs)
    targets = (leaf_targets, mid_targets)
    offsets = (0, leaf_count, leaf_count + leaf_count // 2)
    carried = None
    forward = []
    top_contribution = None
    for height in range(3):
        group_width, within, front_index, member = place_level(
            height, section, row_index, row_count
        )
        inverse = inverses[height]
        panel_rows = panels[height]
        pivot_local = inverse.shape[0]
        pivot_live = live_rows(member, pivot_local, front_counts[offsets[height] + front_index, 0])
        update_live = live_rows(
            member, panel_rows.shape[0], front_counts[offsets[height] + front_index, 1]
        )
        source = sources[height].astype(jnp.float32)
        if carried is not None:
            source = source + carried[:, :pivot_local]
        assembled_local = jnp.where(pivot_live, source, 0.0).astype(jnp.bfloat16)
        gathered = lax.all_gather(assembled_local, "rows", axis=1, tiled=True)
        assembled = share_sections(gathered[:, None, :], height, within).reshape(
            gathered.shape[0], PIVOTS
        )
        solved = jnp.einsum("cp,rp->cr", assembled, inverse, preferred_element_type=jnp.float32)
        solved = jnp.where(pivot_live, solved, 0.0).astype(jnp.bfloat16)
        update = -jnp.einsum("cp,rp->cr", assembled, panel_rows, preferred_element_type=jnp.float32)
        if carried is not None:
            update = carried[:, pivot_local:] + update
        update = jnp.where(update_live, update, 0.0).astype(jnp.bfloat16)
        forward.append(solved)
        if height < 2:
            carried = extend_children(
                update, height, targets[height], section, row_index, row_count
            )
        else:
            top_contribution = update
    solutions = [None, None, None]
    given_rows = outer_solution
    for height in (2, 1, 0):
        group_width, within, front_index, member = place_level(
            height, section, row_index, row_count
        )
        inverse = inverses[height]
        panel_rows = panels[height]
        pivot_local = inverse.shape[0]
        pivot_live = live_rows(member, pivot_local, front_counts[offsets[height] + front_index, 0])
        update_live = live_rows(
            member, panel_rows.shape[0], front_counts[offsets[height] + front_index, 1]
        )
        given_rows = jnp.where(update_live, given_rows, jnp.zeros_like(given_rows))
        partials = jnp.dot(forward[height], inverse, preferred_element_type=jnp.float32) - jnp.dot(
            given_rows, panel_rows, preferred_element_type=jnp.float32
        )
        if height == 0:
            solution = separate_sums(partials, group_width, height, within)
        else:
            solution = separate_sums(partials, group_width, height, within)
        solution = jnp.where(pivot_live, solution, 0.0).astype(jnp.bfloat16)
        solutions[height] = solution
        if height > 0:
            full_local = jnp.concatenate([solution, given_rows], axis=1)
            given_rows = descend_children(
                full_local, height, targets[height - 1], section, row_count, pivot_local
            )
    return (solutions[0], solutions[1], solutions[2], top_contribution)


def solution(mesh):
    placed = (
        P(("leaf", "rows"), None),
        P(("leaf", "rows"), None),
        P(("leaf", "rows"), None),
        P(("leaf", "rows"), None),
        P(("leaf", "rows"), None),
        P(("leaf", "rows"), None),
        P(None, ("leaf", "rows")),
        P(None, ("leaf", "rows")),
        P(None, ("leaf", "rows")),
        P(None, ("leaf", "rows")),
        P(),
        P(),
        P(),
    )
    return jax.shard_map(
        body,
        mesh=mesh,
        in_specs=placed,
        out_specs=(
            P(None, ("leaf", "rows")),
            P(None, ("leaf", "rows")),
            P(None, ("leaf", "rows")),
            P(None, ("leaf", "rows")),
        ),
        check_vma=False,
    )
```

profile of v0, /device:TPU:2, one launch (start us, length us, event | category | flops | bytes accessed | tf_op | source)
XLA Modules:
  0.0 1120.8 jit_solution(15445964068958309150)
XLA Ops:
  7.2 1.5 constant_dynamic-slice_fusion.2
  9.9 0.8 select_convert_fusion.1
  10.7 52.8 %all_gather.9 = bf16[128,2048]{0,1:T(8,128)(2,1)S(1)} all-gather(bf16[128,64]{0,1:T(8,128)(2,1)S(1)} %select_convert_fusion.1), channel_id=1, replica_groups=mesh['leaf'=8,'rows'=32] {'rows'}, dimensions={1}, use_global_device_ids=true | all-gather | bytes 540672 | tf_op jit(solution)/shard_map/all_gather | solution.py:165
  64.7 3.3 fusion.5
  68.2 0.8 all_to_all.84
  69.0 6.1 all-to-all-start
  75.8 10.8 all-to-all-done
  88.5 9.6 copy.158
  98.1 16.8 %reshape.243 = bf16[32,2,2048]{2,1,0:T(2,128)(2,1)} reshape(bf16[16384,2,4]{2,1,0:T(2,128)(2,1)} %bitcast.148) | data formatting | bytes 524288
  114.9 3.9 all-to-all-start.1
  118.8 11.5 %all-to-all-done.1 = bf16[32,2,2048]{2,1,0:T(2,128)(2,1)S(1)} async-done(((bf16[32,2,2048]{2,1,0:T(2,128)(2,1)}), bf16[32,2,2048]{2,1,0:T(2,128)(2,1)S(1)}, u32[]{:S(2)}, u32[]{:S(2)}) %all-to-all-start.1) | async-done | bytes 262176 | tf_op jit(solution)/shard_map/all_to_all | solution.py:80
  130.3 19.1 %reshape.244 = bf16[16384,2,4]{2,1,0:T(2,128)(2,1)} reshape(bf16[32,2,2048]{2,1,0:T(2,128)(2,1)S(1)} %all-to-all-done.1) | data formatting | bytes 524288
  149.4 16.5 %copy.159 = bf16[4,2,16384]{2,0,1:T(4,128)(2,1)S(1)} copy(bf16[4,2,16384]{0,1,2:T(2,128)(2,1)} %bitcast.149) | data formatting | bytes 524288 | tf_op jit(solution)/shard_map/all_to_all | solution.py:80
  168.4 47.3 %all_gather.10 = bf16[128,1024]{0,1:T(8,128)(2,1)S(1)} all-gather(bf16[128,32]{0,1:T(8,128)(2,1)S(1)} %fusion.42), channel_id=1, replica_groups=mesh['leaf'=8,'rows'=32] {'rows'}, dimensions={1}, use_global_device_ids=true | all-gather | bytes 270336 | tf_op jit(solution)/shard_map/all_gather | solution.py:165
  217.0 0.8 collective-permute-done.1
  219.4 5.2 all-to-all-start.2
  224.6 0.8 dynamic-slice_bitcast_fusion
  225.4 10.0 all-to-all-done.2
  237.3 6.6 copy.166
  243.9 16.8 %reshape.245 = bf16[32,2,2048]{2,1,0:T(2,128)(2,1)} reshape(bf16[8192,4,4]{2,1,0:T(4,128)(2,1)} %bitcast.150) | data formatting | bytes 524288
  260.7 3.9 all-to-all-start.3
  264.7 12.0 %all-to-all-done.3 = bf16[32,2,2048]{2,1,0:T(2,128)(2,1)S(1)} async-done(((bf16[32,2,2048]{2,1,0:T(2,128)(2,1)}), bf16[32,2,2048]{2,1,0:T(2,128)(2,1)S(1)}, u32[]{:S(2)}, u32[]{:S(2)}) %all-to-all-start.3) | async-done | bytes 262176 | tf_op jit(solution)/shard_map/all_to_all | solution.py:80
  276.7 19.1 %reshape.246 = bf16[8192,4,4]{2,1,0:T(4,128)(2,1)} reshape(bf16[32,2,2048]{2,1,0:T(2,128)(2,1)S(1)} %all-to-all-done.3) | data formatting | bytes 524288
  295.8 10.9 copy.167
  307.4 0.7 copy.201
  308.8 4.5 collective-permute-done.2
  315.4 41.1 %all_gather.11 = bf16[128,512]{0,1:T(8,128)(2,1)S(1)} all-gather(bf16[128,16]{0,1:T(8,128)(2,1)S(1)} %fusion.48), channel_id=1, replica_groups=mesh['leaf'=8,'rows'=32] {'rows'}, dimensions={1}, use_global_device_ids=true | all-gather | bytes 135168 | tf_op jit(solution)/shard_map/all_gather | solution.py:165
  356.6 1.3 collective-permute-done.4
  359.2 1.6 broadcast_select_fusion.1
  360.7 5.8 collective-permute-done.5
  366.5 1.1 maximum_select_fusion.1
  367.6 1.5 fusion.15
  369.2 1.9 fusion
  371.0 1.0 copy.195
  372.0 213.9 %reduce-scatter.4.cloned.1.call-done = bf16[128,4,16]{0,2,1:T(8,128)(2,1)} async-done(((bf16[128,4,512]{0,2,1:T(8,128)(2,1)}), bf16[128,4,16]{0,2,1:T(8,128)(2,1)}) %reduce-scatter.4.cloned.1.call-update) | async-done | bytes 16400 | tf_op jit(solution)/shard_map/reduce_scatter | solution.py:117
  586.0 0.7 convert.30
  587.3 3.2 collective-permute-done.6
  590.6 1.2 collective-permute-done.7
  591.9 0.8 pad_maximum_fusion.3
  592.8 16.7 %all_to_all.111 = bf16[32,4,256]{2,1,0:T(4,128)(2,1)S(1)} all-to-all(bf16[32,4,256]{2,1,0:T(4,128)(2,1)S(1)} %all_to_all.92), channel_id=1, replica_groups=mesh['leaf'=8,'rows'=32] {'rows'}, dimensions={0} | all-to-all | bytes 131072 | tf_op jit(solution)/shard_map/all_to_all | solution.py:89
  609.5 1.3 collective-permute-done.8
  611.6 5.0 collective-permute-done.9
  618.3 0.9 copy.178
  619.5 0.9 fusion.9
  620.6 0.8 copy.180
  621.3 3.8 all-to-all-start.5
  625.2 2.5 fusion.13
  627.7 8.0 all-to-all-done.5
  636.0 1.8 fusion.1
  637.8 1.0 copy.182
  638.8 211.2 %reduce-scatter.6.cloned.1.call-done = bf16[128,2,32]{0,2,1:T(8,128)(2,1)} async-done(((bf16[128,2,1024]{0,2,1:T(8,128)(2,1)}), bf16[128,2,32]{0,2,1:T(8,128)(2,1)}) %reduce-scatter.6.cloned.1.call-update) | async-done | bytes 16400 | tf_op jit(solution)/shard_map/reduce_scatter | solution.py:117
  850.8 1.1 collective-permute-done.10
  852.8 17.4 %all_to_all.112 = bf16[32,4,512]{2,1,0:T(4,128)(2,1)S(1)} all-to-all(bf16[32,4,512]{2,1,0:T(4,128)(2,1)S(1)} %pad_maximum_fusion.2), channel_id=1, replica_groups=mesh['leaf'=8,'rows'=32] {'rows'}, dimensions={0} | all-to-all | bytes 262144 | tf_op jit(solution)/shard_map/all_to_all | solution.py:89
  870.5 1.3 collective-permute-done.11
  873.4 0.9 copy.187
  874.3 4.6 all-to-all-start.7
  879.2 1.7 fusion.11
  880.9 11.5 %all-to-all-done.7 = bf16[4,32,960]{2,0,1:T(4,128)(2,1)} async-done(((bf16[4,32,960]{2,0,1:T(4,128)(2,1)}), bf16[4,32,960]{2,0,1:T(4,128)(2,1)}, u32[]{:S(2)}, u32[]{:S(2)}) %all-to-all-start.7) | async-done | bytes 245792 | tf_op jit(solution)/shard_map/all_to_all | solution.py:112
  892.4 1.7 all_to_all.102
  894.1 1.8 copy.188
  896.0 4.9 fusion.3
  900.9 2.2 fusion.28
  903.1 209.5 %reduce-scatter.8.cloned.1.call-done = bf16[128,1,64]{0,2,1:T(8,128)(2,1)} async-done(((bf16[128,1,2048]{0,2,1:T(8,128)(2,1)}), bf16[128,1,64]{0,2,1:T(8,128)(2,1)}) %reduce-scatter.8.cloned.1.call-update) | async-done | bytes 16400 | tf_op jit(solution)/shard_map/reduce_scatter | solution.py:117
  1112.6 1.4 fusion.40
  (139 shorter events, 24.6 us)
Async XLA Ops:
  7.2 210.7 %copy-start = (bf16[480,2048]{1,0:T(8,128)(2,1)S(1)}, bf16[480,2048]{1,0:T(8,128)(2,1)}, u32[]{:S(2)}) copy-start(bf16[480,2048]{1,0:T(8,128)(2,1)} %param.16) | copy-start | bytes 5898244
  9.3 0.6 copy-start.6
  63.5 5.5 copy-start.1
  64.2 0.6 copy-start.11
  69.0 17.7 %all-to-all-start = ((bf16[32,4,960]{2,1,0:T(4,128)(2,1)}), bf16[32,4,960]{2,1,0:T(4,128)(2,1)S(1)}, u32[]{:S(2)}, u32[]{:S(2)}) async-start(bf16[32,4,960]{2,1,0:T(4,128)(2,1)} %all_to_all.84), calls=%async_computation | async-start | bytes 524288 | tf_op jit(solution)/shard_map/all_to_all | solution.py:65
  114.9 15.4 %all-to-all-start.1 = ((bf16[32,2,2048]{2,1,0:T(2,128)(2,1)}), bf16[32,2,2048]{2,1,0:T(2,128)(2,1)S(1)}, u32[]{:S(2)}, u32[]{:S(2)}) async-start(bf16[32,2,2048]{2,1,0:T(2,128)(2,1)} %reshape.243), calls=%async_computation.1 | async-start | bytes 524288 | tf_op jit(solution)/shard_map/all_to_all | solution.py:80
  165.9 2.5 copy-start.5
  166.9 1.4 collective-permute-start
  215.7 2.1 collective-permute-start.1
  216.9 20.3 %copy-start.9 = (pred[480]{0:T(512)(128)(4,1)}, pred[480]{0:T(512)(128)(4,1)S(1)}, u32[]{:S(2)}) copy-start(pred[480]{0:T(512)(128)(4,1)S(1)} %add_compare_fusion.1) | copy-start | bytes 1444
  219.4 16.0 %all-to-all-start.2 = ((bf16[32,4,480]{2,1,0:T(4,128)(2,1)}), bf16[32,4,480]{2,1,0:T(4,128)(2,1)S(1)}, u32[]{:S(2)}, u32[]{:S(2)}) async-start(bf16[32,4,480]{2,1,0:T(4,128)(2,1)} %all_to_all.88), calls=%async_computation.2 | async-start | bytes 262144 | tf_op jit(solution)/shard_map/all_to_all | solution.py:65
  225.4 10.9 copy-start.8
  260.7 15.9 %all-to-all-start.3 = ((bf16[32,2,2048]{2,1,0:T(2,128)(2,1)}), bf16[32,2,2048]{2,1,0:T(2,128)(2,1)S(1)}, u32[]{:S(2)}, u32[]{:S(2)}) async-start(bf16[32,2,2048]{2,1,0:T(2,128)(2,1)} %reshape.245), calls=%async_computation.3 | async-start | bytes 524288 | tf_op jit(solution)/shard_map/all_to_all | solution.py:80
  264.6 321.4 %reduce-scatter.4.cloned.1.call-start = ((), (), s32[]{:S(2)}) async-start(), calls=%async_computation.11 | async-start | bytes 540672 | tf_op jit(solution)/shard_map/reduce_scatter | solution.py:117
  306.6 8.7 copy-start.13
  307.3 60.3 %copy-start.3 = (bf16[16,2048]{1,0:T(8,128)(2,1)S(1)}, bf16[16,2048]{1,0:T(8,128)(2,1)}, u32[]{:S(2)}) copy-start(bf16[16,2048]{1,0:T(8,128)(2,1)} %param.17) | copy-start | bytes 196612
  308.1 5.2 collective-permute-start.2
  313.3 1.3 collective-permute-start.3
  314.7 0.7 copy-start.2
  356.5 1.4 collective-permute-start.4
  358.0 8.6 collective-permute-start.5
  359.1 8.5 copy-start.14
  586.7 3.8 collective-permute-start.6
  590.5 45.4 %copy-start.10 = (pred[480]{0:T(512)(128)(4,1)S(1)}, pred[480]{0:T(512)(128)(4,1)}, u32[]{:S(2)}) copy-start(pred[480]{0:T(512)(128)(4,1)} %copy-done.9) | copy-start | bytes 1444
  590.5 1.3 collective-permute-start.7
  591.9 45.9 %copy-start.4 = (bf16[128,16]{0,1:T(8,128)(2,1)}, bf16[128,16]{0,1:T(8,128)(2,1)S(1)}, u32[]{:S(2)}) copy-start(bf16[128,16]{0,1:T(8,128)(2,1)S(1)} %fusion.49) | copy-start | bytes 12292
  609.5 1.3 collective-permute-start.8
  610.9 5.6 collective-permute-start.9
  621.3 14.4 %all-to-all-start.5 = ((bf16[4,32,480]{2,0,1:T(4,128)(2,1)}), bf16[4,32,480]{2,0,1:T(4,128)(2,1)S(1)}, u32[]{:S(2)}, u32[]{:S(2)}) async-start(bf16[4,32,480]{2,0,1:T(4,128)(2,1)} %copy.180), calls=%async_computation.6 | async-start | bytes 262144 | tf_op jit(solution)/shard_map/all_to_all | solution.py:112
  625.2 224.8 %reduce-scatter.6.cloned.1.call-start = ((), (), s32[]{:S(2)}) async-start(), calls=%async_computation.12 | async-start | bytes 540672 | tf_op jit(solution)/shard_map/reduce_scatter | solution.py:117
  638.8 240.4 %copy-start.7 = (pred[64]{0:T(512)(128)(4,1)S(1)}, pred[64]{0:T(512)(128)(4,1)}, u32[]{:S(2)}) copy-start(pred[64]{0:T(512)(128)(4,1)} %copy-done.6) | copy-start | bytes 196
  850.7 1.2 collective-permute-start.10
  870.4 1.4 collective-permute-start.11
  871.9 24.1 %copy-start.12 = (pred[960]{0:T(1024)(128)(4,1)S(1)}, pred[960]{0:T(1024)(128)(4,1)}, u32[]{:S(2)}) copy-start(pred[960]{0:T(1024)(128)(4,1)} %copy-done.11) | copy-start | bytes 2884
  874.3 18.1 %all-to-all-start.7 = ((bf16[4,32,960]{2,0,1:T(4,128)(2,1)}), bf16[4,32,960]{2,0,1:T(4,128)(2,1)}, u32[]{:S(2)}, u32[]{:S(2)}) async-start(bf16[4,32,960]{2,0,1:T(4,128)(2,1)} %copy.187), calls=%async_computation.9 | async-start | bytes 524288 | tf_op jit(solution)/shard_map/all_to_all | solution.py:112
  878.9 233.7 %reduce-scatter.8.cloned.1.call-start = ((), (), s32[]{:S(2)}) async-start(), calls=%async_computation.13 | async-start | bytes 540672 | tf_op jit(solution)/shard_map/reduce_scatter | solution.py:117
  880.8 20.1 %copy-start.15 = (pred[240]{0:T(512)(128)(4,1)S(1)}, pred[240]{0:T(512)(128)(4,1)}, u32[]{:S(2)}) copy-start(pred[240]{0:T(512)(128)(4,1)} %copy-done.14) | copy-start | bytes 724
Sparse Core Ops, SparseCore 0:
  372.2 213.7 reduce-scatter.3
  638.9 211.0 reduce-scatter.5
  901.0 211.5 reduce-scatter.7
where the time goes:
time: 1130 us; the launch traced here: 1120 us
  waiting for transfers between devices  725 us (64%)
  blocking collectives  175 us (15%)
  local copies, waits for them, and re-layouts  139 us (12%)
  starting transfers between devices  31.1 us (3%)
  matrix products  22.3 us (2%)
  between operations  14.9 us (1%)
  other arithmetic  13.2 us (1%)
    reduce_scatter x3, waiting for transfers between devices, separate_sums(): lax.psum_scatter(shaped.astype(jnp.bfloat16), 'rows', scatter_dimension=2...  635 us
    all_gather x3, blocking collectives, body(): gathered = lax.all_gather(assembled_local, 'rows', axis=1, tiled=True)  141 us
    unnamed x42, local copies, waits for them, and re-layouts  75.2 us
    all_to_all x2, blocking collectives, descend_children(): lax.all_to_all(full_local, 'rows', split_axis=0, concat_axis=1, tiled=True)  34.1 us
    all_to_all x2, local copies, waits for them, and re-layouts, extend_children(): lax.all_to_all(joined.astype(jnp.bfloat16), 'rows', split_axis=2, concat_...  27.3 us
    ppermute x12, waiting for transfers between devices, from_partner(): return lax.ppermute(value, axis, pairs)  26.3 us
    all_to_all x2, waiting for transfers between devices, extend_children(): lax.all_to_all(joined.astype(jnp.bfloat16), 'rows', split_axis=2, concat_...  23.5 us
  transfers between devices with their start and end apart: 21, of which 21 were waited for; matrix products, arithmetic and copies ran while one was open for 1% of the time, Pallas kernels for 0%

commit v1 on v0

--- a/solution.py
+++ b/solution.py
@@ -77,8 +77,14 @@
     pivot_side = flattened[:, :PIVOTS].reshape(narrow, parent_width, row_count, -1)
     update_side = flattened[:, PIVOTS:].reshape(narrow, parent_width, row_count, -1)
     joined = jnp.concatenate([pivot_side, update_side], axis=3).reshape(narrow, parent_width, -1)
-    returned = lax.all_to_all(
-        joined.astype(jnp.bfloat16), "rows", split_axis=2, concat_axis=0, tiled=True
+    returned = jnp.concatenate(
+        lax.all_to_all(
+            jnp.stack(jnp.split(joined.astype(jnp.bfloat16), lax.axis_size("rows"), axis=2)),
+            "rows",
+            0,
+            0,
+        ),
+        axis=0,
     ).astype(joined.dtype)
     return total_sections(returned, height + 1, section % parent_width)
 

time: 1130 us -> 1010 us (0.89)
  waiting for transfers between devices: 725 us -> 653 us
  local copies, waits for them, and re-layouts: 139 us -> 83.8 us
    reduce_scatter x3 -> x2, waiting for transfers between devices: 635 us -> 421 us  [separate_sums(): lax.psum_scatter(shaped.astype(jnp.bfloat16), 'rows', scatter_dimension=2...]
    unnamed x3 -> x4, waiting for transfers between devices: 0.05 us -> 144 us
    unnamed x42 -> x106, local copies, waits for them, and re-layouts: 75.2 us -> 39.4 us
    all_to_all x2 -> x0, local copies, waits for them, and re-layouts: 27.3 us -> none  [extend_children(): lax.all_to_all(joined.astype(jnp.bfloat16), 'rows', split_axis=2, concat_...]
    concatenate x2 -> x0, local copies, waits for them, and re-layouts: 16.2 us -> none  [extend_children(): jnp.concatenate([pivot_side, update_side], axis=3)]
  transfers between devices with their start and end apart: 21 -> 21, of which waited for: 21 -> 21; matrix products, arithmetic and copies ran while one was open for 1% -> 2% of each run, Pallas kernels for 0% -> 0%
where the time goes in v1:
time: 1010 us
  waiting for transfers between devices  653 us (65%)
  blocking collectives  174 us (17%)
  local copies, waits for them, and re-layouts  83.8 us (8%)
  starting transfers between devices  31.5 us (3%)
  matrix products  25 us (2%)
  other arithmetic  22.4 us (2%)
  between operations  15.3 us (2%)
    reduce_scatter x2, waiting for transfers between devices, separate_sums(): lax.psum_scatter(shaped.astype(jnp.bfloat16), 'rows', scatter_dimension=2...  421 us
    unnamed x4, waiting for transfers between devices  144 us
    all_gather x3, blocking collectives, body(): gathered = lax.all_gather(assembled_local, 'rows', axis=1, tiled=True)  141 us
    unnamed x106, local copies, waits for them, and re-layouts  39.4 us
    all_to_all x2, blocking collectives, descend_children(): lax.all_to_all(full_local, 'rows', split_axis=0, concat_axis=1, tiled=True)  33.1 us
    ppermute x12, waiting for transfers between devices, from_partner(): return lax.ppermute(value, axis, pairs)  24.3 us
    all_to_all x2, waiting for transfers between devices, extend_children(): lax.all_to_all(jnp.stack(jnp.split(joined.astype(jnp.bfloat16), lax.axis_...  23.2 us
    all_to_all x2, waiting for transfers between devices, extend_children(): lax.all_to_all(update, 'rows', split_axis=0, concat_axis=1, tiled=True)  20.8 us
  transfers between devices with their start and end apart: 21, of which 21 were waited for; matrix products, arithmetic and copies ran while one was open for 2% of the time, Pallas kernels for 0%

profile of v1, /device:TPU:2, one launch (start us, length us, event | category | flops | bytes accessed | tf_op | source)
XLA Modules:
  0.0 1005.0 jit_solution(10365799077689417231)
XLA Ops:
  7.2 1.6 constant_dynamic-slice_fusion.1
  10.7 52.8 %all_gather.9 = bf16[128,2048]{0,1:T(8,128)(2,1)S(1)} all-gather(bf16[128,64]{0,1:T(8,128)(2,1)S(1)} %select_convert_fusion.1), channel_id=1, replica_groups=mesh['leaf'=8,'rows'=32] {'rows'}, dimensions={1}, use_global_device_ids=true | all-gather | bytes 540672 | tf_op jit(solution)/shard_map/all_gather | solution.py:171
  64.2 3.3 fusion.4
  68.5 6.1 all-to-all-start
  75.3 10.8 %all-to-all-done = bf16[32,4,960]{2,1,0:T(4,128)(2,1)S(1)} async-done(((bf16[32,4,960]{2,1,0:T(4,128)(2,1)}), bf16[32,4,960]{2,1,0:T(4,128)(2,1)S(1)}, u32[]{:S(2)}, u32[]{:S(2)}) %all-to-all-start) | async-done | bytes 245792 | tf_op jit(solution)/shard_map/all_to_all | solution.py:65
  107.4 3.9 all-to-all-start.1
  111.3 11.5 %all-to-all-done.1 = bf16[32,4,2,512]{3,2,1,0:T(2,128)(2,1)S(1)} async-done(((bf16[32,4,2,512]{3,2,1,0:T(2,128)(2,1)}), bf16[32,4,2,512]{3,2,1,0:T(2,128)(2,1)S(1)}, u32[]{:S(2)}, u32[]{:S(2)}) %all-to-all-start.1) | async-done | bytes 262176 | tf_op jit(solution)/shard_map/all_to_all | solution.py:81
  125.0 1.3 convert_add_fusion
  126.5 47.3 %all_gather.10 = bf16[128,1024]{0,1:T(8,128)(2,1)S(1)} all-gather(bf16[128,32]{0,1:T(8,128)(2,1)S(1)} %fusion.41), channel_id=1, replica_groups=mesh['leaf'=8,'rows'=32] {'rows'}, dimensions={1}, use_global_device_ids=true | all-gather | bytes 270336 | tf_op jit(solution)/shard_map/all_gather | solution.py:171
  175.5 1.1 maximum_select_fusion
  178.2 5.2 all-to-all-start.2
  184.1 10.0 all-to-all-done.2
  196.5 1.1 pad_maximum_fusion.1
  217.0 4.6 all-to-all-start.3
  221.9 11.7 %all-to-all-done.3 = bf16[32,4,4,256]{3,2,1,0:T(4,128)(2,1)} async-done(((bf16[32,4,4,256]{3,2,1,0:T(4,128)(2,1)}), bf16[32,4,4,256]{3,2,1,0:T(4,128)(2,1)}, u32[]{:S(2)}, u32[]{:S(2)}) %all-to-all-start.3) | async-done | bytes 262176 | tf_op jit(solution)/shard_map/all_to_all | solution.py:81
  233.5 1.0 copy_convert_fusion
  234.6 1.1 copy.1862
  235.7 1.2 reshape.231
  237.6 1.7 copy.1864
  240.5 1.1 copy.1863
  241.6 2.9 collective-permute-done.2
  247.0 41.2 %all_gather.11 = bf16[128,512]{0,1:T(8,128)(2,1)S(1)} all-gather(bf16[128,16]{0,1:T(8,128)(2,1)S(1)} %fusion.47), channel_id=1, replica_groups=mesh['leaf'=8,'rows'=32] {'rows'}, dimensions={1}, use_global_device_ids=true | all-gather | bytes 135168 | tf_op jit(solution)/shard_map/all_gather | solution.py:171
  288.2 1.3 collective-permute-done.4
  290.9 1.6 broadcast_select_fusion.1
  292.5 5.7 collective-permute-done.5
  298.1 1.4 maximum_select_fusion.1
  299.5 2.4 fusion.14
  302.0 2.7 fusion
  304.6 2.2 convert_element_type.191
  306.9 2.2 copy.1865
  310.3 144.4 %all-reduce.3.cloned.1.call-done = bf16[128,4,512]{0,1,2:T(4,128)(2,1)} async-done(((bf16[128,4,512]{0,1,2:T(4,128)(2,1)}), bf16[128,4,512]{0,1,2:T(4,128)(2,1)}) %all-reduce.3.cloned.1.call-update) | async-done | bytes 524304
  456.1 3.1 collective-permute-done.6
  459.3 1.2 collective-permute-done.7
  461.1 1.5 pad_maximum_fusion.3
  462.6 1.6 copy.1867
  464.2 1.5 all_to_all.84
  465.7 15.5 %all_to_all.103 = bf16[32,4,256]{2,1,0:T(4,128)(2,1)S(1)} all-to-all(bf16[32,4,256]{2,1,0:T(4,128)(2,1)} %all_to_all.84), channel_id=1, replica_groups=mesh['leaf'=8,'rows'=32] {'rows'}, dimensions={0} | all-to-all | bytes 131072 | tf_op jit(solution)/shard_map/all_to_all | solution.py:95
  481.2 1.3 collective-permute-done.8
  483.3 4.9 collective-permute-done.9
  490.1 2.1 reshape.223
  492.3 1.6 copy.1873
  493.8 1.1 reshape.222
  494.9 1.1 maximum_bitcast_fusion
  496.0 1.5 fusion.8
  497.5 1.8 convert_element_type.200
  499.2 1.7 copy.1875
  500.9 4.7 all-to-all-start.5
  505.7 2.5 fusion.12
  508.2 7.9 all-to-all-done.5
  517.9 1.9 fusion.1
  520.8 211.2 %reduce-scatter.3.cloned.1.call-done = bf16[128,2,32]{0,2,1:T(8,128)(2,1)} async-done(((bf16[128,2,1024]{0,2,1:T(8,128)(2,1)}), bf16[128,2,32]{0,2,1:T(8,128)(2,1)}) %reduce-scatter.3.cloned.1.call-update) | async-done | bytes 16400 | tf_op jit(solution)/shard_map/reduce_scatter | solution.py:123
  734.9 17.6 %all_to_all.104 = bf16[32,4,512]{2,1,0:T(4,128)(2,1)S(1)} all-to-all(bf16[32,4,512]{2,1,0:T(4,128)(2,1)S(1)} %pad_maximum_fusion.2), channel_id=1, replica_groups=mesh['leaf'=8,'rows'=32] {'rows'}, dimensions={0} | all-to-all | bytes 262144 | tf_op jit(solution)/shard_map/all_to_all | solution.py:95
  752.5 1.3 collective-permute-done.11
  755.5 2.1 reshape.226
  758.6 1.1 maximum_bitcast_fusion.1
  759.6 1.7 fusion.7
  761.3 1.2 convert_element_type.209
  763.4 3.9 all-to-all-start.7
  767.3 2.2 fusion.10
  769.5 11.3 %all-to-all-done.7 = bf16[4,32,960]{2,0,1:T(4,128)(2,1)S(1)} async-done(((bf16[4,32,960]{2,0,1:T(4,128)(2,1)}), bf16[4,32,960]{2,0,1:T(4,128)(2,1)S(1)}, u32[]{:S(2)}, u32[]{:S(2)}) %all-to-all-start.7) | async-done | bytes 245792 | tf_op jit(solution)/shard_map/all_to_all | solution.py:118
  781.1 3.2 fusion.2
  785.4 2.2 fusion.27
  787.7 209.4 %reduce-scatter.5.cloned.1.call-done = bf16[128,1,64]{0,2,1:T(8,128)(2,1)} async-done(((bf16[128,1,2048]{0,2,1:T(8,128)(2,1)}), bf16[128,1,64]{0,2,1:T(8,128)(2,1)}) %reduce-scatter.5.cloned.1.call-update) | async-done | bytes 16400 | tf_op jit(solution)/shard_map/reduce_scatter | solution.py:123
  997.1 1.4 fusion.39
  (205 shorter events, 75.3 us)
Async XLA Ops:
  7.2 169.5 %copy-start = (bf16[480,2048]{1,0:T(8,128)(2,1)S(1)}, bf16[480,2048]{1,0:T(8,128)(2,1)}, u32[]{:S(2)}) copy-start(bf16[480,2048]{1,0:T(8,128)(2,1)} %param.16) | copy-start | bytes 5898244
  9.4 0.6 copy-start.10
  64.2 4.3 copy-start.15
  68.5 17.7 %all-to-all-start = ((bf16[32,4,960]{2,1,0:T(4,128)(2,1)}), bf16[32,4,960]{2,1,0:T(4,128)(2,1)S(1)}, u32[]{:S(2)}, u32[]{:S(2)}) async-start(bf16[32,4,960]{2,1,0:T(4,128)(2,1)} %all_to_all.76), calls=%async_computation | async-start | bytes 524288 | tf_op jit(solution)/shard_map/all_to_all | solution.py:65
  75.3 11.9 %copy-start.6 = (s32[1,240]{1,0:T(1,128)}, s32[1,240]{1,0:T(1,128)S(1)}, u32[]{:S(2)}) copy-start(s32[1,240]{1,0:T(1,128)S(1)} %constant_dynamic-slice_fusion.3) | copy-start | bytes 2884
  86.2 40.3 %copy-start.7 = (bf16[128,32]{0,1:T(8,128)(2,1)S(1)}, bf16[128,32]{0,1:T(8,128)(2,1)}, u32[]{:S(2)}) copy-start(bf16[128,32]{0,1:T(8,128)(2,1)} %param.20) | copy-start | bytes 24580
  107.4 15.4 %all-to-all-start.1 = ((bf16[32,4,2,512]{3,2,1,0:T(2,128)(2,1)}), bf16[32,4,2,512]{3,2,1,0:T(2,128)(2,1)S(1)}, u32[]{:S(2)}, u32[]{:S(2)}) async-start(bf16[32,4,2,512]{3,2,1,0:T(2,128)(2,1)} %constant_dynamic-update-slice_fusion), calls=%async_computation.1 | async-start | bytes 524288 | tf_op jit(solution)/shard_map/all_to_all | solution.py:81
  123.2 1.8 collective-permute-start
  124.0 71.1 %copy-start.8 = (pred[32]{0:T(512)(128)(4,1)}, pred[32]{0:T(512)(128)(4,1)S(1)}, u32[]{:S(2)}) copy-start(pred[32]{0:T(512)(128)(4,1)S(1)} %add_compare_fusion.4) | copy-start | bytes 100
  173.8 1.7 collective-permute-start.1
  174.6 8.8 copy-start.13
  178.2 16.0 %all-to-all-start.2 = ((bf16[32,4,480]{2,1,0:T(4,128)(2,1)}), bf16[32,4,480]{2,1,0:T(4,128)(2,1)S(1)}, u32[]{:S(2)}, u32[]{:S(2)}) async-start(bf16[32,4,480]{2,1,0:T(4,128)(2,1)} %all_to_all.80), calls=%async_computation.2 | async-start | bytes 262144 | tf_op jit(solution)/shard_map/all_to_all | solution.py:65
  184.1 53.5 %copy-start.12 = (s32[120]{0:T(128)}, s32[120]{0:T(128)S(1)}, u32[]{:S(2)}) copy-start(s32[120]{0:T(128)S(1)} %dynamic-slice_bitcast_fusion) | copy-start | bytes 1444
  196.5 50.4 %copy-start.16 = (bf16[128,16]{0,1:T(8,128)(2,1)S(1)}, bf16[128,16]{0,1:T(8,128)(2,1)}, u32[]{:S(2)}) copy-start(bf16[128,16]{0,1:T(8,128)(2,1)} %param.21) | copy-start | bytes 12292
  217.0 16.6 %all-to-all-start.3 = ((bf16[32,4,4,256]{3,2,1,0:T(4,128)(2,1)}), bf16[32,4,4,256]{3,2,1,0:T(4,128)(2,1)}, u32[]{:S(2)}, u32[]{:S(2)}) async-start(bf16[32,4,4,256]{3,2,1,0:T(4,128)(2,1)} %constant_dynamic-update-slice_fusion.32), calls=%async_computation.3 | async-start | bytes 524288 | tf_op jit(solution)/shard_map/all_to_all | solution.py:81
  221.6 233.1 %all-reduce.3.cloned.1.call-start = ((), (), s32[]{:S(2)}) async-start(), calls=%async_computation.12 | async-start | bytes 1048576
  239.3 5.3 collective-permute-start.2
  245.5 1.3 collective-permute-start.3
  246.9 41.3 %copy-start.3 = (f32[128,256]{0,1:T(8,128)}, f32[128,256]{0,1:T(8,128)S(1)}, u32[]{:S(2)}) copy-start(f32[128,256]{0,1:T(8,128)S(1)} %add_bitcast_fusion) | copy-start | bytes 393220
  288.2 1.4 collective-permute-start.4
  289.6 2.9 copy-start.2
  289.6 8.6 collective-permute-start.5
  290.9 1.6 copy-start.17
  292.5 16.6 %copy-start.19 = (u32[256]{0:T(256)S(1)}, u32[256]{0:T(256)}, u32[]{:S(2)}) copy-start(u32[256]{0:T(256)} %constant.277) | copy-start | bytes 3076
  455.5 3.7 collective-permute-start.6
  459.2 1.2 collective-permute-start.7
  460.5 0.6 copy-start.5
  481.2 1.3 collective-permute-start.8
  482.5 5.6 collective-permute-start.9
  500.9 231.9 %copy-start.14 = (pred[480]{0:T(512)(128)(4,1)S(1)}, pred[480]{0:T(512)(128)(4,1)}, u32[]{:S(2)}) copy-start(pred[480]{0:T(512)(128)(4,1)} %copy-done.13) | copy-start | bytes 1444
  500.9 15.2 %all-to-all-start.5 = ((bf16[4,32,480]{2,0,1:T(4,128)(2,1)}), bf16[4,32,480]{2,0,1:T(4,128)(2,1)}, u32[]{:S(2)}, u32[]{:S(2)}) async-start(bf16[4,32,480]{2,0,1:T(4,128)(2,1)} %copy.1875), calls=%async_computation.5 | async-start | bytes 262144 | tf_op jit(solution)/shard_map/all_to_all | solution.py:118
  505.6 228.3 %copy-start.9 = (pred[32]{0:T(512)(128)(4,1)S(1)}, pred[32]{0:T(512)(128)(4,1)}, u32[]{:S(2)}) copy-start(pred[32]{0:T(512)(128)(4,1)} %copy-done.8) | copy-start | bytes 100
  505.6 226.4 %reduce-scatter.3.cloned.1.call-start = ((), (), s32[]{:S(2)}) async-start(), calls=%async_computation.10 | async-start | bytes 540672 | tf_op jit(solution)/shard_map/reduce_scatter | solution.py:123
  520.8 246.5 %copy-start.1 = (bf16[64,2048]{1,0:T(8,128)(2,1)S(1)}, bf16[64,2048]{1,0:T(8,128)(2,1)}, u32[]{:S(2)}) copy-start(bf16[64,2048]{1,0:T(8,128)(2,1)} %param.13) | copy-start | bytes 786436
  732.8 1.2 collective-permute-start.10
  752.5 1.3 collective-permute-start.11
  763.4 17.4 %all-to-all-start.7 = ((bf16[4,32,960]{2,0,1:T(4,128)(2,1)}), bf16[4,32,960]{2,0,1:T(4,128)(2,1)S(1)}, u32[]{:S(2)}, u32[]{:S(2)}) async-start(bf16[4,32,960]{2,0,1:T(4,128)(2,1)} %copy.1882), calls=%async_computation.8 | async-start | bytes 524288 | tf_op jit(solution)/shard_map/all_to_all | solution.py:118
  767.3 229.9 %reduce-scatter.5.cloned.1.call-start = ((), (), s32[]{:S(2)}) async-start(), calls=%async_computation.11 | async-start | bytes 540672 | tf_op jit(solution)/shard_map/reduce_scatter | solution.py:123
  780.9 4.5 copy-start.4
  780.9 4.5 copy-start.18
  781.1 216.0 %copy-start.11 = (pred[64]{0:T(512)(128)(4,1)S(1)}, pred[64]{0:T(512)(128)(4,1)}, u32[]{:S(2)}) copy-start(pred[64]{0:T(512)(128)(4,1)} %copy-done.10) | copy-start | bytes 196
Sparse Core Ops, SparseCore 0:
  309.2 145.5 all-reduce.2
  521.0 211.0 reduce-scatter.2
  785.5 211.5 reduce-scatter.4
